TPU v7x, 256 devices: a whole 4x4x8 slice. The times are simulated.
256 devices in a mesh: owner: 8 (over y, core), group: 32 (over z, x).
Axes of the slice: x: 4, y: 4, z: 8, core: 2. Of those that a mesh axis runs over, the one named last changes fastest.
Arguments:
- amplitudes: bfloat16 [1024, 32768], P('group', 'owner'), may hold values from -6 to 6
- integrals: bfloat16 [32768, 32768], P('owner', 'group'), may hold values from -0.09375 to 0.09375
- occ_irrep: int32 [100], replicated, may hold values from 0 to 7
- vir_irrep: int32 [1200], replicated, may hold values from 0 to 7, as said below
- cd_list: int32 [2, 32768], P(None, 'owner'), may hold values from 0 to 1199
- ab_list: int32 [2, 32768], P(None, 'group'), may hold values from 0 to 1199, as said below
Outputs:
- ladder: bfloat16 [1024, 32768], P('owner', 'group')
Inputs may be any that keep to these rules, and one draw needn't show every extreme that they name: `vir_irrep`: irrep labels of D2h; each of the 8 labels occurs. `occ_irrep`: irrep labels of D2h. `cd_list`: indices of virtual orbitals. `ab_list`: indices of virtual orbitals; the residual pairs of each index of group form 8 consecutive blocks of 128 pairs, and every pair (a,b) of block k has vir_irrep[a] XOR vir_irrep[b] == k.
All inputs are finite; a program needn't handle non-finite values.
Results may differ from a plain program's by a relative error of at most 0.001.
Values may be sent and summed in bfloat16 or wider, within the bound.
No kernel may reach another device: no remote copies, remote signals or barrier semaphores. Data moves between devices by JAX's collectives and lax.ppermute only.
A program may use at most 64 MiB of HBM per device.

v0:
```python
import jax
import jax.numpy as jnp
from jax import lax
from jax.sharding import PartitionSpec as P


def label_lookup(indices, table):
    count = table.shape[0]
    columns = jnp.arange(count, dtype=jnp.int32)
    onehot = (indices[:, None] == columns[None, :]).astype(jnp.bfloat16)
    values = jnp.dot(
        onehot, table.astype(jnp.bfloat16)[:, None], preferred_element_type=jnp.float32
    )
    return values[:, 0].astype(jnp.int32)


def pair_irreps(pair_list, table):
    length = pair_list.shape[1]
    both = label_lookup(pair_list.reshape(2 * length), table)
    return jnp.bitwise_xor(both[:length], both[length:])


def local(amplitudes, integrals, occ_irrep, vir_irrep, cd_list, ab_list):
    sym_cd = pair_irreps(cd_list, vir_irrep)
    sym_ab = pair_irreps(ab_list, vir_irrep)
    total_pairs = amplitudes.shape[0] * lax.axis_size("group")
    occupied = occ_irrep.shape[0]
    rows = jnp.arange(total_pairs, dtype=jnp.int32)
    row_pairs = jnp.concatenate([rows // occupied, rows % occupied])
    both_occ = label_lookup(row_pairs, occ_irrep)
    sym_ij = jnp.bitwise_xor(both_occ[:total_pairs], both_occ[total_pairs:])
    weights = jnp.where(
        sym_cd[:, None] == sym_ab[None, :], integrals, jnp.zeros((), integrals.dtype)
    )
    gathered = lax.all_gather(amplitudes, "group", axis=0, tiled=True)
    selected = jnp.where(
        sym_ij[:, None] == sym_cd[None, :], gathered, jnp.zeros((), gathered.dtype)
    )
    product = jnp.dot(selected, weights, preferred_element_type=jnp.float32)
    reduced = lax.psum_scatter(product, "owner", scatter_dimension=0, tiled=True)
    return reduced.astype(jnp.bfloat16)


def solution(mesh):
    return jax.shard_map(
        local,
        mesh=mesh,
        in_specs=(
            P("group", "owner"),
            P("owner", "group"),
            P(),
            P(),
            P(None, "owner"),
            P(None, "group"),
        ),
        out_specs=P("owner", "group"),
        check_vma=False,
    )
```

profile of v0, /device:TPU:2, one launch (start us, length us, event | category | flops | bytes accessed | tf_op | source)
XLA Modules:
  0.0 173.8 jit_solution(6140189908563980151)
XLA Ops:
  6.5 0.0 all-gather.2.cloned.1.call-start
  6.5 0.7 all-gather.2.cloned.1.call-update
  7.3 0.0 reduce-scatter.2.cloned.1.call-start
  7.3 0.7 convert_element_type.24
  8.0 0.7 copy.10
  8.7 2.2 %fusion.2 = f32[1,2048]{1,0:T(1,128)S(1)} fusion(bf16[1200,1]{0,1:T(2,128)(2,1)S(1)} %reshape.21, s32[2048]{0:T(1024)S(1)} %bitcast.20), kind=kOutput, calls=%fused_computation.6 | convolution fusion | flops 7372800 | bytes 18784 | tf_op jit(solution)/shard_map/dot_general | solution.py:11
  10.9 1.1 fusion.11
  12.1 0.8 copy.7
  12.8 5.8 %fusion = f32[1,8192]{1,0:T(1,128)S(1)} fusion(bf16[1200,1]{0,1:T(2,128)(2,1)S(1)} %reshape.21, s32[8192]{0:T(1024)S(1)} %bitcast.16), kind=kOutput, calls=%fused_computation.1 | convolution fusion | flops 29491200 | bytes 67936 | tf_op jit(solution)/shard_map/dot_general | solution.py:11
  18.7 90.8 %all-gather.2.cloned.1.call-done = bf16[1024,4096]{1,0:T(8,128)(2,1)} async-done(((bf16[32,4096]{1,0:T(8,128)(2,1)}), bf16[1024,4096]{1,0:T(8,128)(2,1)}) %all-gather.2.cloned.1.call-update) | async-done | bytes 8388624 | tf_op jit(solution)/shard_map/all_gather | solution.py:35
  109.5 16.7 %fusion.3 = f32[1024,1024]{1,0:T(8,128)} fusion(bf16[1024,4096]{1,0:T(8,128)(2,1)} %all-gather.2.cloned.1.call-done, bf16[4096,1024]{1,0:T(8,128)(2,1)} %param.7, s32[1024]{0:T(1024)S(1)} %slice_xor_fusion.1, s32[4096]{0:T(1024)S(1)} %slice_xor_fusion, s32[1024]{0:T(1024)S(1)} %slice_xor_fusion.2), kind=kOutput, calls=%fused_computation.7 | convolution fusion | flops 8606711808 | bytes 20996096 | tf_op jit(solution)/shard_map/dot_general | solution.py:39
  126.1 0.0 reduce-scatter.2.cloned.1.call-update
  126.2 39.1 %reduce-scatter.2.cloned.1.call-done = f32[128,1024]{1,0:T(8,128)} async-done(((f32[1024,1024]{1,0:T(8,128)}), f32[128,1024]{1,0:T(8,128)}) %reduce-scatter.2.cloned.1.call-update) | async-done | bytes 524304 | tf_op jit(solution)/shard_map/reduce_scatter | solution.py:40
  165.2 1.8 %convert_element_type.27 = bf16[128,1024]{1,0:T(8,128)(2,1)} convert(f32[128,1024]{1,0:T(8,128)} %reduce-scatter.2.cloned.1.call-done) | non-fusion elementwise | flops 131072 | bytes 786432 | tf_op jit(solution)/shard_map/convert_element_type | solution.py:41
  (9 shorter events, 0.1 us)
Async XLA Ops:
  6.5 103.0 %all-gather.2.cloned.1.call-start = ((), (), s32[]{:S(2)}) async-start(), calls=%async_computation.1 | async-start | bytes 8650752 | tf_op jit(solution)/shard_map/all_gather | solution.py:35
  7.3 158.0 %reduce-scatter.2.cloned.1.call-start = ((), (), s32[]{:S(2)}) async-start(), calls=%async_computation.2 | async-start | bytes 4718592 | tf_op jit(solution)/shard_map/reduce_scatter | solution.py:40
Sparse Core Ops, SparseCore 0:
  9.9 99.5 all-gather.1
  126.3 38.8 reduce-scatter.1
where the time goes:
time: 174 us
  waiting for transfers between devices  131 us (75%)
  matrix products  25.8 us (15%)
  between operations  13.4 us (8%)
  other arithmetic  2.53 us (1%)
    all_gather x1, waiting for transfers between devices, local(): gathered = lax.all_gather(amplitudes, 'group', axis=0, tiled=True)  90.8 us
    reduce_scatter x1, waiting for transfers between devices, local(): lax.psum_scatter(product, 'owner', scatter_dimension=0, tiled=True)  39.1 us
    dot_general x1, matrix products, local(): product = jnp.dot(selected, weights, preferred_element_type=jnp.float32)  16.7 us
    dot_general x3, matrix products, label_lookup(): jnp.dot(onehot, table.astype(jnp.bfloat16)[:, None], preferred_element_ty...  9.14 us
  transfers between devices with their start and end apart: 2, of which 2 were waited for; matrix products, arithmetic and copies ran while one was open for 7% of the time, Pallas kernels for 0%

commit v1 on v0

--- a/solution.py
+++ b/solution.py
@@ -2,6 +2,13 @@
 import jax.numpy as jnp
 from jax import lax
 from jax.sharding import PartitionSpec as P
+
+hold_figure_all = lambda z, array_axis: jnp.concatenate(
+    lax.all_to_all(
+        jnp.stack([z] * lax.axis_size("group")), axis_name="group", split_axis=0, concat_axis=0
+    ),
+    axis=array_axis,
+)
 
 
 def label_lookup(indices, table):
@@ -32,7 +39,7 @@
     weights = jnp.where(
         sym_cd[:, None] == sym_ab[None, :], integrals, jnp.zeros((), integrals.dtype)
     )
-    gathered = lax.all_gather(amplitudes, "group", axis=0, tiled=True)
+    gathered = hold_figure_all(amplitudes, 0)
     selected = jnp.where(
         sym_ij[:, None] == sym_cd[None, :], gathered, jnp.zeros((), gathered.dtype)
     )

time: 174 us -> 284 us (1.63)
  waiting for transfers between devices: 131 us -> 226 us
  starting transfers between devices: 0.04 us -> 11.8 us
  local copies, waits for them, and re-layouts: 1.47 us -> 5.25 us
    all_to_all x0 -> x1, waiting for transfers between devices: none -> 182 us  [lax.all_to_all(jnp.stack([z] * lax.axis_size('group')), axis_name='group'...]
    all_gather x1 -> x0, waiting for transfers between devices: 90.8 us -> none  [local(): gathered = lax.all_gather(amplitudes, 'group', axis=0, tiled=True)]
    all_to_all x0 -> x1, starting transfers between devices: none -> 11.8 us  [lax.all_to_all(jnp.stack([z] * lax.axis_size('group')), axis_name='group'...]
    reduce_scatter x1, waiting for transfers between devices: 39.1 us -> 44.9 us  [local(): lax.psum_scatter(product, 'owner', scatter_dimension=0, tiled=True)]
    another operation x0 -> x1, local copies, waits for them, and re-layouts: none -> 5.22 us  [jnp.stack([z] * lax.axis_size('group'))]
  transfers between devices with their start and end apart: 2 -> 2, of which waited for: 2 -> 2; matrix products, arithmetic and copies ran while one was open for 7% -> 3% of each run, Pallas kernels for 0% -> 0%
where the time goes in v1:
time: 284 us
  waiting for transfers between devices  226 us (80%)
  matrix products  25.3 us (9%)
  between operations  13.5 us (5%)
  starting transfers between devices  11.8 us (4%)
  local copies, waits for them, and re-layouts  5.25 us (2%)
    all_to_all x1, waiting for transfers between devices, lax.all_to_all(jnp.stack([z] * lax.axis_size('group')), axis_name='group'...  182 us
    reduce_scatter x1, waiting for transfers between devices, local(): lax.psum_scatter(product, 'owner', scatter_dimension=0, tiled=True)  44.9 us
    dot_general x1, matrix products, local(): product = jnp.dot(selected, weights, preferred_element_type=jnp.float32)  16.7 us
    all_to_all x1, starting transfers between devices, lax.all_to_all(jnp.stack([z] * lax.axis_size('group')), axis_name='group'...  11.8 us
    dot_general x3, matrix products, label_lookup(): jnp.dot(onehot, table.astype(jnp.bfloat16)[:, None], preferred_element_ty...  8.59 us
  transfers between devices with their start and end apart: 2, of which 2 were waited for; matrix products, arithmetic and copies ran while one was open for 3% of the time, Pallas kernels for 0%

profile of v1, /device:TPU:2, one launch (start us, length us, event | category | flops | bytes accessed | tf_op | source)
XLA Modules:
  0.0 284.2 jit_solution(10886669695736260065)
XLA Ops:
  6.5 5.2 %stack.2 = bf16[32,32,4096]{2,1,0:T(8,128)(2,1)} broadcast(bf16[32,4096]{1,0:T(8,128)(2,1)} %param.6), dimensions={1,2} | broadcast | bytes 8650752 | tf_op jit(solution)/shard_map/stack | solution.py:8
  11.8 0.0 copy-start.1
  11.8 0.0 copy-start.2
  11.8 0.0 copy-start
  11.8 11.8 %all-to-all-start = ((bf16[32,32,4096]{2,1,0:T(8,128)(2,1)}), bf16[32,32,4096]{2,1,0:T(8,128)(2,1)}, u32[]{:S(2)}, u32[]{:S(2)}) async-start(bf16[32,32,4096]{2,1,0:T(8,128)(2,1)} %stack.2), calls=%async_computation | async-start | bytes 16777216 | tf_op jit(solution)/shard_map/all_to_all | solution.py:7
  23.6 0.0 copy-start.3
  23.6 0.0 reduce-scatter.2.cloned.1.call-start
  23.6 0.0 copy-done.1
  23.7 0.0 copy-done.2
  23.7 2.3 fusion.2
  26.0 0.0 copy-done
  26.0 5.8 %fusion = f32[1,8192]{1,0:T(1,128)S(1)} fusion(bf16[1200,1]{0,1:T(2,128)(2,1)S(1)} %reshape.27, s32[8192]{0:T(1024)S(1)} %bitcast.17), kind=kOutput, calls=%fused_computation.1 | convolution fusion | flops 29491200 | bytes 67936 | tf_op jit(solution)/shard_map/dot_general | solution.py:18
  31.9 0.0 copy-done.3
  31.9 0.5 fusion.11
  32.4 181.5 %all-to-all-done = bf16[32,32,4096]{2,1,0:T(8,128)(2,1)} async-done(((bf16[32,32,4096]{2,1,0:T(8,128)(2,1)}), bf16[32,32,4096]{2,1,0:T(8,128)(2,1)}, u32[]{:S(2)}, u32[]{:S(2)}) %all-to-all-start) | async-done | bytes 8388640 | tf_op jit(solution)/shard_map/all_to_all | solution.py:7
  213.9 16.7 %fusion.3 = f32[1024,1024]{1,0:T(8,128)} fusion(bf16[1024,4096]{1,0:T(8,128)(2,1)} %bitcast.3, bf16[4096,1024]{1,0:T(8,128)(2,1)} %param.7, s32[1024]{0:T(1024)S(1)} %slice_xor_fusion.1, s32[4096]{0:T(1024)S(1)} %slice_xor_fusion, s32[1024]{0:T(1024)S(1)} %slice_xor_fusion.2), kind=kOutput, calls=%fused_computation.7 | convolution fusion | flops 8606711808 | bytes 20996096 | tf_op jit(solution)/shard_map/dot_general | solution.py:46
  230.6 0.0 reduce-scatter.2.cloned.1.call-update
  230.6 44.9 %reduce-scatter.2.cloned.1.call-done = f32[128,1024]{1,0:T(8,128)} async-done(((f32[1024,1024]{1,0:T(8,128)}), f32[128,1024]{1,0:T(8,128)}) %reduce-scatter.2.cloned.1.call-update) | async-done | bytes 524304 | tf_op jit(solution)/shard_map/reduce_scatter | solution.py:47
  275.5 1.8 convert_element_type.27
  (12 shorter events, 0.1 us)
Async XLA Ops:
  11.8 11.9 %copy-start.1 = (s32[1200]{0:T(1024)S(1)}, s32[1200]{0:T(1024)}, u32[]{:S(2)}) copy-start(s32[1200]{0:T(1024)} %param.9) | copy-start | bytes 14404
  11.8 11.9 %copy-start.2 = (s32[2,1024]{1,0:T(2,128)S(1)}, s32[2,1024]{1,0:T(2,128)}, u32[]{:S(2)}) copy-start(s32[2,1024]{1,0:T(2,128)} %param.11) | copy-start | bytes 24580
  11.8 14.3 %copy-start = (s32[2,4096]{1,0:T(2,128)S(1)}, s32[2,4096]{1,0:T(2,128)}, u32[]{:S(2)}) copy-start(s32[2,4096]{1,0:T(2,128)} %param.10) | copy-start | bytes 98308
  11.8 202.1 %all-to-all-start = ((bf16[32,32,4096]{2,1,0:T(8,128)(2,1)}), bf16[32,32,4096]{2,1,0:T(8,128)(2,1)}, u32[]{:S(2)}, u32[]{:S(2)}) async-start(bf16[32,32,4096]{2,1,0:T(8,128)(2,1)} %stack.2), calls=%async_computation | async-start | bytes 16777216 | tf_op jit(solution)/shard_map/all_to_all | solution.py:7
  23.6 8.3 %copy-start.3 = (s32[100]{0:T(128)S(1)}, s32[100]{0:T(128)}, u32[]{:S(2)}) copy-start(s32[100]{0:T(128)} %param.8) | copy-start | bytes 1204
  23.6 252.0 %reduce-scatter.2.cloned.1.call-start = ((), (), s32[]{:S(2)}) async-start(), calls=%async_computation.2 | async-start | bytes 4718592 | tf_op jit(solution)/shard_map/reduce_scatter | solution.py:47
Sparse Core Ops, SparseCore 0:
  230.7 44.7 reduce-scatter.1
